TPU v7x, 32 devices: a whole 2x2x4 slice. The times are simulated.
32 devices in a mesh: space: 8 (over z, x), freq: 4 (over y, core).
Axes of the slice: x: 2, y: 2, z: 4, core: 2. Of those that a mesh axis runs over, the one named last changes fastest.
Arguments:
- u_velocity: bfloat16 [2176, 16, 512], P(None, 'space', 'freq'), may hold values from -6 to 6
- v_velocity: bfloat16 [2176, 16, 512], P(None, 'space', 'freq'), may hold values from -6 to 6
- cell_weights: float32 [16, 512], P('space', 'freq'), may hold values from 0.25 to 4
- block_offsets: int32 [16], replicated, may hold values from 0 to 1920
- triads: int32 [64, 2], replicated, may hold values from 0 to 63
Outputs:
- eigen_values: float32 [64, 2], replicated
- mode_fields: float32 [64, 2, 16, 512], P(None, None, 'space', 'freq')
Inputs may be any that keep to these rules, and one draw needn't show every extreme that they name: `triads`: k and l are each below 64, so k + l is below 128.
All inputs are finite; a program needn't handle non-finite values.
Results may differ from a plain program's by a relative error of at most 0.012.
Values may be sent and summed in bfloat16 or wider, within the bound.
No kernel may reach another device: no remote copies, remote signals or barrier semaphores. Data moves between devices by JAX's collectives and lax.ppermute only.
A program may use at most 64 MiB of HBM per device.

v0:
```python
import math
import jax
import jax.numpy as jnp
from jax import lax
from jax.sharding import PartitionSpec as P

NFFT = 256
POW = 4


def with_halo(cells, sides, width):
    for axis, dim in sides:
        count = lax.axis_size(axis)
        ends = count - 1
        head = lax.slice_in_dim(cells, 0, width, axis=dim)
        tail = lax.slice_in_dim(cells, cells.shape[dim] - width, cells.shape[dim], axis=dim)
        cells = jnp.concatenate(
            [
                lax.ppermute(tail, axis, [(i, (i + 1) % count) for i in range(ends)]),
                cells,
                lax.ppermute(head, axis, [((i + 1) % count, i) for i in range(ends)]),
            ],
            axis=dim,
        )
    return cells


def make_table(length):
    half_len = length // 2
    times_idx = jnp.arange(length, dtype=jnp.int32)
    freq_idx = jnp.arange(half_len, dtype=jnp.int32)
    phases = freq_idx[:, None] * times_idx[None, :] % length
    angles = phases.astype(jnp.float32) * (2.0 * math.pi / length)
    window = 0.5 - 0.5 * jnp.cos(times_idx.astype(jnp.float32) * (2.0 * math.pi / length))
    scaling = 1.0 / jnp.sqrt(jnp.sum(window * window))
    transform = jnp.concatenate([jnp.cos(angles) * scaling, -jnp.sin(angles) * scaling], axis=0)
    return (window, transform.astype(jnp.bfloat16))


def spectra(vorticity, offsets):
    window, transform = make_table(NFFT)
    fluct = vorticity - jnp.mean(vorticity, axis=0, keepdims=True)
    blocks = jax.vmap(lambda start: lax.dynamic_slice_in_dim(fluct, start, NFFT, 0))(offsets)
    windowed = (blocks * window[None, :, None, None]).astype(jnp.bfloat16)
    return jnp.einsum("ft,btxy->bfxy", transform, windowed, preferred_element_type=jnp.float32)


def cross_terms(spectrum, weights, triads):
    half_len = spectrum.shape[1] // 2
    real_part = spectrum[:, :half_len]
    imag_part = spectrum[:, half_len:]
    target = triads[:, 0] + triads[:, 1]
    first_re = jnp.take(real_part, triads[:, 0], axis=1)
    first_im = jnp.take(imag_part, triads[:, 0], axis=1)
    second_re = jnp.take(real_part, triads[:, 1], axis=1)
    second_im = jnp.take(imag_part, triads[:, 1], axis=1)
    target_re = jnp.take(real_part, target, axis=1)
    target_im = jnp.take(imag_part, target, axis=1)
    prod_re = (first_re * second_re - first_im * second_im) * weights
    prod_im = (first_re * second_im + first_im * second_re) * weights
    high = lax.Precision.HIGHEST
    cross_re = jnp.einsum("btxy,ctxy->tbc", prod_re, target_re, precision=high) + jnp.einsum(
        "btxy,ctxy->tbc", prod_im, target_im, precision=high
    )
    cross_im = jnp.einsum("btxy,ctxy->tbc", prod_re, target_im, precision=high) - jnp.einsum(
        "btxy,ctxy->tbc", prod_im, target_re, precision=high
    )
    return (jnp.stack([cross_re, cross_im], axis=1), target_re, target_im)


def leading(matrices):
    high = lax.Precision.HIGHEST
    mat_re = matrices[:, 0]
    mat_im = matrices[:, 1]
    vec_re = jnp.full(mat_re.shape[:2], 1.0 / math.sqrt(mat_re.shape[1]), jnp.float32)
    vec_im = jnp.zeros(mat_re.shape[:2], jnp.float32)

    def apply(part_re, part_im):
        out_re = jnp.einsum("tbc,tc->tb", mat_re, part_re, precision=high) - jnp.einsum(
            "tbc,tc->tb", mat_im, part_im, precision=high
        )
        out_im = jnp.einsum("tbc,tc->tb", mat_re, part_im, precision=high) + jnp.einsum(
            "tbc,tc->tb", mat_im, part_re, precision=high
        )
        return (out_re, out_im)

    for repeat in range(POW):
        out_re, out_im = apply(vec_re, vec_im)
        length = jnp.sqrt(jnp.sum(out_re * out_re + out_im * out_im, axis=1, keepdims=True))
        vec_re = out_re / length
        vec_im = out_im / length
    out_re, out_im = apply(vec_re, vec_im)
    value_re = jnp.sum(vec_re * out_re + vec_im * out_im, axis=1)
    value_im = jnp.sum(vec_re * out_im - vec_im * out_re, axis=1)
    return (jnp.stack([vec_re, vec_im], axis=1), jnp.stack([value_re, value_im], axis=1))


def on_device(u_velocity, v_velocity, cell_weights, block_offsets, triads):
    u_part = with_halo(u_velocity, (("freq", 2),), 1).astype(jnp.float32)
    v_part = with_halo(v_velocity, (("space", 1),), 1).astype(jnp.float32)
    vorticity = 0.5 * (v_part[:, 2:, :] - v_part[:, :-2, :]) - 0.5 * (
        u_part[:, :, 2:] - u_part[:, :, :-2]
    )
    spectrum = spectra(vorticity, block_offsets)
    partial_value, target_re, target_im = cross_terms(spectrum, cell_weights, triads)
    cells = vorticity.shape[1] * vorticity.shape[2] * lax.axis_size("space") * lax.axis_size("freq")
    scaling = 1.0 / (partial_value.shape[2] * math.sqrt(cells))
    mine = lax.psum_scatter(partial_value, "freq", scatter_dimension=0, tiled=True)
    mine = lax.psum(mine, "space") * scaling
    own_vectors, own_values = leading(mine)
    vectors, values = (
        lax.all_gather(own_vectors, "freq", axis=0, tiled=True),
        lax.all_gather(own_values, "freq", axis=0, tiled=True),
    )
    high = lax.Precision.HIGHEST
    vec_re = vectors[:, 0]
    vec_im = vectors[:, 1]
    mode_re = jnp.einsum("tb,btxy->txy", vec_re, target_re, precision=high) - jnp.einsum(
        "tb,btxy->txy", vec_im, target_im, precision=high
    )
    mode_im = jnp.einsum("tb,btxy->txy", vec_re, target_im, precision=high) + jnp.einsum(
        "tb,btxy->txy", vec_im, target_re, precision=high
    )
    return (values, jnp.stack([mode_re, mode_im], axis=1))


def solution(mesh):
    return jax.shard_map(
        on_device,
        mesh=mesh,
        in_specs=(P(None, "space", "freq"), P(None, "space", "freq"), P("space", "freq"), P(), P()),
        out_specs=(P(), P(None, None, "space", "freq")),
        check_vma=False,
    )
```

profile of v0, /device:TPU:0, one launch (start us, length us, event | category | flops | bytes accessed | tf_op | source)
XLA Modules:
  0.0 192.5 jit_solution(13298839978467539383)
XLA Ops:
  7.2 3.7 %fusion.92 = (bf16[2176,1,128]{2,1,0:T(2,128)(2,1)S(1)}, bf16[2176,1,128]{2,1,0:T(2,128)(2,1)S(1)}) fusion(bf16[2176,2,128]{2,1,0:T(2,128)(2,1)} %param.8), kind=kLoop, calls=%fused_computation.155 | loop fusion | bytes 2228224 | tf_op jit(solution)/shard_map/slice | solution.py:16
  11.8 5.7 %collective-permute-start = (bf16[2176,1,128]{2,0,1:T(8,128)(2,1)}, bf16[2176,1,128]{2,0,1:T(8,128)(2,1)}, u32[]{:S(2)}, u32[]{:S(2)}) collective-permute-start(bf16[2176,1,128]{2,0,1:T(8,128)(2,1)} %copy.121), channel_id=1, source_target_pairs={{0,4},{4,8},{8,12},{12,16},{16,20},{20,24},{24,28},{1,5},{5,9},{9,... | collective-permute-start | bytes 1671176 | tf_op jit(solution)/shard_map/ppermute | solution.py:19
  19.7 2.1 %fusion.93 = (bf16[2176,2,1]{2,1,0:T(2,128)(2,1)S(1)}, bf16[2176,2,1]{2,1,0:T(2,128)(2,1)S(1)}) fusion(bf16[2176,2,128]{2,1,0:T(2,128)(2,1)S(1)} %copy-done.2), kind=kLoop, calls=%fused_computation.156 | loop fusion | bytes 34816 | tf_op jit(solution)/shard_map/slice | solution.py:16
  29.4 1.6 copy.66
  31.0 1.6 copy.67
  32.7 6.0 %maximum_convert_fusion.1 = f32[2176,2,130]{2,1,0:T(2,128)S(1)} fusion(bf16[2176,2,1]{2,1,0:T(2,128)(2,1)S(1)} %copy.67, bf16[2176,2,128]{2,1,0:T(2,128)(2,1)S(1)} %copy-done.2, bf16[2176,2,1]{2,1,0:T(2,128)(2,1)S(1)} %copy.66), kind=kLoop, calls=%fused_computation.15 | loop fusion | flops 3394560 | bytes 3394560 | tf_op jit(solution)/shard_map/convert_element_type | solution.py:99
  38.7 2.1 %collective-permute-done = bf16[2176,1,128]{2,0,1:T(8,128)(2,1)} collective-permute-done((bf16[2176,1,128]{2,0,1:T(8,128)(2,1)}, bf16[2176,1,128]{2,0,1:T(8,128)(2,1)}, u32[]{:S(2)}, u32[]{:S(2)}) %collective-permute-start) | collective-permute-done | bytes 557088 | tf_op jit(solution)/shard_map/ppermute | solution.py:19
  40.8 5.6 %copy.62 = bf16[2176,1,128]{2,1,0:T(2,128)(2,1)S(1)} copy(bf16[2176,1,128]{2,0,1:T(8,128)(2,1)} %collective-permute-done) | data formatting | bytes 1114112 | tf_op jit(solution)/shard_map/ppermute | solution.py:19
  46.4 5.6 %copy.63 = bf16[2176,1,128]{2,1,0:T(2,128)(2,1)S(1)} copy(bf16[2176,1,128]{2,0,1:T(8,128)(2,1)} %collective-permute-done.1) | data formatting | bytes 1114112 | tf_op jit(solution)/shard_map/ppermute | solution.py:21
  52.0 3.5 %maximum_convert_fusion = f32[2176,4,128]{2,1,0:T(4,128)S(1)} fusion(bf16[2176,1,128]{2,1,0:T(2,128)(2,1)S(1)} %copy.63, bf16[2176,2,128]{2,1,0:T(2,128)(2,1)S(1)} %copy-done.3, bf16[2176,1,128]{2,1,0:T(2,128)(2,1)S(1)} %copy.62), kind=kLoop, calls=%fused_computation.14 | loop fusion | flops 6684672 | bytes 6684672 | tf_op jit(solution)/shard_map/convert_element_type | solution.py:100
  55.6 3.1 %fusion.89 = (f32[2,128]{1,0:T(2,128)S(1)}, f32[2176,2,128]{2,1,0:T(2,128)S(1)}) fusion(f32[2176,2,130]{2,1,0:T(2,128)S(1)} %maximum_convert_fusion.1, f32[2176,4,128]{2,1,0:T(4,128)S(1)} %maximum_convert_fusion), kind=kLoop, calls=%fused_computation.153 | loop fusion | flops 3342080 | bytes 11142144 | tf_op jit(solution)/shard_map/reduce_sum | solution.py:42
  58.9 6.5 %gather_fusion = f32[16,256,2,128]{3,2,1,0:T(2,128)} fusion(f32[2176,2,128]{2,1,0:T(2,128)S(1)} %bitcast.240, s32[16]{0:T(128)S(1)} %fusion.79), kind=kCustom, calls=%fused_computation.6 | custom fusion | bytes 8388800 | tf_op jit(solution)/shard_map/vmap()/gather | solution.py:43
  65.3 3.0 %convolution_bitcast_fusion = f32[16,256,2,128]{1,3,2,0:T(8,128)S(1)} fusion(f32[16,256,2,128]{3,2,1,0:T(2,128)} %gather_fusion, f32[256]{0:T(256)S(1)} %multiply_subtract_fusion, bf16[128,256]{1,0:T(8,128)(2,1)S(1)} %get-tuple-element.47, bf16[128,256]{1,0:T(8,128)(2,1)S(1)} %get-tuple-element.48), kind=kOutput, calls=%fused_computation.16 | convolution fusion | flops 539230208 | bytes 8520704 | tf_op jit(solution)/shard_map/ft,btxy->bfxy/dot_general | solution.py:45
  68.4 2.5 %fusion.91 = (f32[16,128,2,128]{1,3,2,0:T(8,128)}, f32[16,128,2,128]{1,3,2,0:T(8,128)}) fusion(f32[16,256,2,128]{1,3,2,0:T(8,128)S(1)} %convolution_bitcast_fusion), kind=kLoop, calls=%fused_computation.154 | loop fusion | bytes 8388608 | tf_op jit(solution)/shard_map/slice | solution.py:50
  70.9 2.4 %copy.70 = f32[16,128,2,128]{3,0,2,1:T(8,128)S(1)} copy(f32[16,128,2,128]{1,3,2,0:T(8,128)} %get-tuple-element.27) | data formatting | bytes 4194304 | tf_op jit(solution)/shard_map/slice | solution.py:50
  73.3 3.9 %copy.72 = f32[16,128,2,128]{3,0,2,1:T(8,128)} copy(f32[16,128,2,128]{1,3,2,0:T(8,128)} %get-tuple-element.28) | data formatting | bytes 4194304 | tf_op jit(solution)/shard_map/slice | solution.py:51
  78.8 3.2 %gather_fusion.4 = f32[64,16,2,128]{3,1,2,0:T(8,128)} fusion(f32[16,128,2,128]{3,0,2,1:T(8,128)} %copy.72, s32[1024]{0:T(1024)S(1)} %get-tuple-element.50), kind=kCustom, calls=%fused_computation.3.clone | custom fusion | bytes 2097408 | tf_op jit(solution)/shard_map/jit(_take)/gather | solution.py:56
  83.6 3.3 %gather_fusion.3 = f32[64,16,2,128]{3,1,2,0:T(8,128)} fusion(f32[16,128,2,128]{3,0,2,1:T(8,128)} %copy.72, s32[1024]{0:T(1024)S(1)} %pad_clamp_fusion.2), kind=kCustom, calls=%fused_computation.2.clone | custom fusion | bytes 2097408 | tf_op jit(solution)/shard_map/jit(_take)/gather | solution.py:54
  87.6 2.3 %gather_fusion.5 = f32[64,16,2,128]{3,1,2,0:T(8,128)S(1)} fusion(f32[16,128,2,128]{3,0,2,1:T(8,128)} %copy-done, s32[1024]{0:T(1024)S(1)} %get-tuple-element.49), kind=kCustom, calls=%fused_computation.4.clone | custom fusion | bytes 2097408 | tf_op jit(solution)/shard_map/jit(_take)/gather | solution.py:57
  89.9 2.4 %fusion.23 = (f32[16,64,2,128]{3,0,2,1:T(8,128)S(1)}, f32[16,64,2,128]{3,0,2,1:T(8,128)S(1)}) fusion(f32[64,16,2,128]{3,1,2,0:T(8,128)} %gather_fusion.4, f32[64,16,2,128]{3,1,2,0:T(8,128)} %gather_fusion.3, f32[64,16,2,128]{3,1,2,0:T(8,128)S(1)} %copy-done.4, f32[64,16,2,128]{3,1,2,0:T(8,128)} %gather_fusion.1, f32[2,128]{1,0:T(2,128)S(1)} %copy-done.5, ...), kind=kLoop, calls=%fused_computation.43 | loop fusion | flops 3145728 | bytes 6292608 | tf_op jit(solution)/shard_map/mul | solution.py:59
  98.5 22.9 %reduce-scatter.4.cloned.1.call-done = f32[16,512]{1,0:T(8,128)} async-done(((f32[64,512]{1,0:T(8,128)}), f32[16,512]{1,0:T(8,128)}) %reduce-scatter.4.cloned.1.call-update) | async-done | bytes 32784
  122.4 40.6 %psum.7 = f32[16,2,16,16]{3,2,0,1:T(8,128)S(1)} all-reduce(f32[16,2,16,16]{3,2,0,1:T(8,128)S(1)} %copy.120), channel_id=1, replica_groups=mesh['space'=8,'freq'=4] {'space'}, use_global_device_ids=true, to_apply=%region_3.5 | all-reduce | flops 8192 | bytes 65536 | tf_op jit(solution)/shard_map/psum | solution.py:109
  169.2 5.2 %all_gather.7 = f32[64,2,16]{2,0,1:T(8,128)S(1)} all-gather(f32[16,2,16]{2,0,1:T(8,128)S(1)} %pad_maximum_fusion.2), channel_id=1, replica_groups=mesh['space'=8,'freq'=4] {'freq'}, dimensions={0}, use_global_device_ids=true | all-gather | bytes 10240 | tf_op jit(solution)/shard_map/all_gather | solution.py:112
  179.1 5.1 %all-gather = f32[4,16,2]{1,2,0:T(2,128)S(1)} all-gather(f32[1,16,2]{1,2,0:T(2,128)S(1)} %maximum_bitcast_fusion.2), channel_id=1, replica_groups=mesh['space'=8,'freq'=4] {'freq'}, dimensions={0}, use_global_device_ids=true | all-gather | bytes 640 | tf_op jit(solution)/shard_map/all_gather | solution.py:113
  (98 shorter events, 33.3 us)
Async XLA Ops:
  7.2 114.3 %reduce-scatter.4.cloned.1.call-start = ((), (), s32[]{:S(2)}) async-start(), calls=%async_computation.1 | async-start | bytes 163840
  10.9 8.8 %copy-start.2 = (bf16[2176,2,128]{2,1,0:T(2,128)(2,1)S(1)}, bf16[2176,2,128]{2,1,0:T(2,128)(2,1)}, u32[]{:S(2)}) copy-start(bf16[2176,2,128]{2,1,0:T(2,128)(2,1)} %param.7) | copy-start | bytes 3342340
  11.8 29.0 %collective-permute-start = (bf16[2176,1,128]{2,0,1:T(8,128)(2,1)}, bf16[2176,1,128]{2,0,1:T(8,128)(2,1)}, u32[]{:S(2)}, u32[]{:S(2)}) collective-permute-start(bf16[2176,1,128]{2,0,1:T(8,128)(2,1)} %copy.121), channel_id=1, source_target_pairs={{0,4},{4,8},{8,12},{12,16},{16,20},{20,24},{24,28},{1,5},{5,9},{9,... | collective-permute-start | bytes 1671176 | tf_op jit(solution)/shard_map/ppermute | solution.py:19
  18.4 28.0 %collective-permute-start.1 = (bf16[2176,1,128]{2,0,1:T(8,128)(2,1)}, bf16[2176,1,128]{2,0,1:T(8,128)(2,1)}, u32[]{:S(2)}, u32[]{:S(2)}) collective-permute-start(bf16[2176,1,128]{2,0,1:T(8,128)(2,1)} %copy.122), channel_id=1, source_target_pairs={{4,0},{8,4},{12,8},{16,12},{20,16},{24,20},{28,24},{5,1},{9,5},{13... | collective-permute-start | bytes 1671176 | tf_op jit(solution)/shard_map/ppermute | solution.py:21
  21.8 6.3 %copy-start.7 = (s32[16]{0:T(128)S(1)}, s32[16]{0:T(128)}, u32[]{:S(2)}) copy-start(s32[16]{0:T(128)} %param.10) | copy-start | bytes 196
  21.8 7.5 %copy-start.6 = (s32[64,2]{0,1:T(2,128)S(1)}, s32[64,2]{0,1:T(2,128)}, u32[]{:S(2)}) copy-start(s32[64,2]{0,1:T(2,128)} %param.11) | copy-start | bytes 1540
  23.1 6.3 %collective-permute-start.2 = (bf16[2176,2,1]{0,1,2:T(2,128)(2,1)S(1)}, bf16[2176,2,1]{0,1,2:T(2,128)(2,1)S(1)}, u32[]{:S(2)}, u32[]{:S(2)}) collective-permute-start(bf16[2176,2,1]{0,1,2:T(2,128)(2,1)S(1)} %copy.123), channel_id=1, source_target_pairs={{0,1},{1,2},{2,3},{4,5},{5,6},{6,7},{8,9},{9,10},{10,11},{12,13},{... | collective-permute-start | bytes 26120 | tf_op jit(solution)/shard_map/ppermute | solution.py:19
  25.9 5.1 %collective-permute-start.3 = (bf16[2176,2,1]{0,1,2:T(2,128)(2,1)S(1)}, bf16[2176,2,1]{0,1,2:T(2,128)(2,1)S(1)}, u32[]{:S(2)}, u32[]{:S(2)}) collective-permute-start(bf16[2176,2,1]{0,1,2:T(2,128)(2,1)S(1)} %copy.124), channel_id=1, source_target_pairs={{1,0},{2,1},{3,2},{5,4},{6,5},{7,6},{9,8},{10,9},{11,10},{13,12},{... | collective-permute-start | bytes 26120 | tf_op jit(solution)/shard_map/ppermute | solution.py:21
  38.7 13.3 %copy-start.3 = (bf16[2176,2,128]{2,1,0:T(2,128)(2,1)S(1)}, bf16[2176,2,128]{2,1,0:T(2,128)(2,1)}, u32[]{:S(2)}) copy-start(bf16[2176,2,128]{2,1,0:T(2,128)(2,1)} %param.8) | copy-start | bytes 3342340
  73.3 8.7 %copy-start = (f32[16,128,2,128]{3,0,2,1:T(8,128)}, f32[16,128,2,128]{3,0,2,1:T(8,128)S(1)}, u32[]{:S(2)}) copy-start(f32[16,128,2,128]{3,0,2,1:T(8,128)S(1)} %copy.70) | copy-start | bytes 6291460
  83.6 3.4 %copy-start.1 = (f32[16,128,2,128]{3,0,2,1:T(8,128)S(1)}, f32[16,128,2,128]{3,0,2,1:T(8,128)}, u32[]{:S(2)}) copy-start(f32[16,128,2,128]{3,0,2,1:T(8,128)} %copy.72) | copy-start | bytes 6291460
  86.9 3.0 %copy-start.5 = (f32[2,128]{1,0:T(2,128)S(1)}, f32[2,128]{1,0:T(2,128)}, u32[]{:S(2)}) copy-start(f32[2,128]{1,0:T(2,128)} %param.9) | copy-start | bytes 3076
  87.6 2.3 %copy-start.4 = (f32[64,16,2,128]{3,1,2,0:T(8,128)S(1)}, f32[64,16,2,128]{3,1,2,0:T(8,128)}, u32[]{:S(2)}) copy-start(f32[64,16,2,128]{3,1,2,0:T(8,128)} %gather_fusion.2) | copy-start | bytes 3145732
Sparse Core Ops, SparseCore 0:
  98.6 22.7 reduce-scatter.3
where the time goes:
time: 193 us
  local copies, waits for them, and re-layouts  55.6 us (29%)
  blocking collectives  50.9 us (26%)
  waiting for transfers between devices  25.1 us (13%)
  other arithmetic  18.2 us (9%)
  matrix products  17.5 us (9%)
  between operations  15.3 us (8%)
  starting transfers between devices  9.92 us (5%)
    psum x1, blocking collectives, on_device(): mine = lax.psum(mine, 'space') * scaling  40.6 us
    unnamed x2, waiting for transfers between devices  23 us
    unnamed x26, local copies, waits for them, and re-layouts  7.42 us
    ppermute x2, local copies, waits for them, and re-layouts, with_halo(): lax.ppermute(head, axis, [((i + 1) % count, i) for i in range(ends)])  7.22 us
    ppermute x2, local copies, waits for them, and re-layouts, with_halo(): lax.ppermute(tail, axis, [(i, (i + 1) % count) for i in range(ends)])  7.22 us
    ppermute x2, starting transfers between devices, with_halo(): lax.ppermute(tail, axis, [(i, (i + 1) % count) for i in range(ends)])  7.13 us
    gather x1, local copies, waits for them, and re-layouts, spectra(): lax.dynamic_slice_in_dim(fluct, start, NFFT, 0)  6.47 us
    convert_element_type x1, other arithmetic, on_device(): u_part = with_halo(u_velocity, (('freq', 2),), 1).astype(jnp.float32)  5.99 us
  transfers between devices with their start and end apart: 5, of which 2 were waited for; matrix products, arithmetic and copies ran while one was open for 11% of the time, Pallas kernels for 0%

commit v1 on v0

--- a/solution.py
+++ b/solution.py
@@ -106,7 +106,7 @@
     cells = vorticity.shape[1] * vorticity.shape[2] * lax.axis_size("space") * lax.axis_size("freq")
     scaling = 1.0 / (partial_value.shape[2] * math.sqrt(cells))
     mine = lax.psum_scatter(partial_value, "freq", scatter_dimension=0, tiled=True)
-    mine = lax.psum(mine, "space") * scaling
+    mine = jnp.sum(lax.all_gather(mine, "space"), axis=0) * scaling
     own_vectors, own_values = leading(mine)
     vectors, values = (
         lax.all_gather(own_vectors, "freq", axis=0, tiled=True),

time: 193 us -> 200 us (1.036)
  blocking collectives: 50.9 us -> 55.7 us
    all_gather x0 -> x1, blocking collectives: none -> 45.4 us  [on_device(): mine = jnp.sum(lax.all_gather(mine, 'space'), axis=0) * scaling]
    psum x1 -> x0, blocking collectives: 40.6 us -> none  [on_device(): mine = lax.psum(mine, 'space') * scaling]
    unnamed x26 -> x22, local copies, waits for them, and re-layouts: 7.42 us -> 7.4 us
where the time goes in v1:
time: 200 us; the launch traced here: 199 us
  local copies, waits for them, and re-layouts  55.9 us (28%)
  blocking collectives  55.7 us (28%)
  waiting for transfers between devices  25.1 us (13%)
  other arithmetic  20 us (10%)
  matrix products  17.5 us (9%)
  between operations  15.3 us (8%)
  starting transfers between devices  9.91 us (5%)
    all_gather x1, blocking collectives, on_device(): mine = jnp.sum(lax.all_gather(mine, 'space'), axis=0) * scaling  45.4 us
    unnamed x2, waiting for transfers between devices  23 us
    unnamed x22, local copies, waits for them, and re-layouts  7.4 us
    ppermute x2, local copies, waits for them, and re-layouts, with_halo(): lax.ppermute(head, axis, [((i + 1) % count, i) for i in range(ends)])  7.22 us
    ppermute x2, local copies, waits for them, and re-layouts, with_halo(): lax.ppermute(tail, axis, [(i, (i + 1) % count) for i in range(ends)])  7.22 us
    ppermute x2, starting transfers between devices, with_halo(): lax.ppermute(tail, axis, [(i, (i + 1) % count) for i in range(ends)])  7.12 us
    gather x1, local copies, waits for them, and re-layouts, spectra(): lax.dynamic_slice_in_dim(fluct, start, NFFT, 0)  6.46 us
    convert_element_type x1, other arithmetic, on_device(): u_part = with_halo(u_velocity, (('freq', 2),), 1).astype(jnp.float32)  5.99 us
  transfers between devices with their start and end apart: 5, of which 2 were waited for; matrix products, arithmetic and copies ran while one was open for 11% of the time, Pallas kernels for 0%

profile of v1, /device:TPU:0, one launch (start us, length us, event | category | flops | bytes accessed | tf_op | source)
XLA Modules:
  0.0 199.3 jit_solution(6470622125032625136)
XLA Ops:
  7.2 3.7 %fusion.92 = (bf16[2176,1,128]{2,1,0:T(2,128)(2,1)S(1)}, bf16[2176,1,128]{2,1,0:T(2,128)(2,1)S(1)}) fusion(bf16[2176,2,128]{2,1,0:T(2,128)(2,1)} %param.8), kind=kLoop, calls=%fused_computation.155 | loop fusion | bytes 2228224 | tf_op jit(solution)/shard_map/slice | solution.py:16
  11.8 5.7 %collective-permute-start = (bf16[2176,1,128]{2,0,1:T(8,128)(2,1)}, bf16[2176,1,128]{2,0,1:T(8,128)(2,1)}, u32[]{:S(2)}, u32[]{:S(2)}) collective-permute-start(bf16[2176,1,128]{2,0,1:T(8,128)(2,1)} %copy.121), channel_id=1, source_target_pairs={{0,4},{4,8},{8,12},{12,16},{16,20},{20,24},{24,28},{1,5},{5,9},{9,... | collective-permute-start | bytes 1671176 | tf_op jit(solution)/shard_map/ppermute | solution.py:19
  19.7 2.1 %fusion.93 = (bf16[2176,2,1]{2,1,0:T(2,128)(2,1)S(1)}, bf16[2176,2,1]{2,1,0:T(2,128)(2,1)S(1)}) fusion(bf16[2176,2,128]{2,1,0:T(2,128)(2,1)S(1)} %copy-done.1), kind=kLoop, calls=%fused_computation.156 | loop fusion | bytes 34816 | tf_op jit(solution)/shard_map/slice | solution.py:16
  32.7 6.0 %maximum_convert_fusion.1 = f32[2176,2,130]{2,1,0:T(2,128)S(1)} fusion(bf16[2176,2,1]{2,1,0:T(2,128)(2,1)S(1)} %copy.67, bf16[2176,2,128]{2,1,0:T(2,128)(2,1)S(1)} %copy-done.1, bf16[2176,2,1]{2,1,0:T(2,128)(2,1)S(1)} %copy.66), kind=kLoop, calls=%fused_computation.15 | loop fusion | flops 3394560 | bytes 3394560 | tf_op jit(solution)/shard_map/convert_element_type | solution.py:99
  38.7 2.1 %collective-permute-done = bf16[2176,1,128]{2,0,1:T(8,128)(2,1)} collective-permute-done((bf16[2176,1,128]{2,0,1:T(8,128)(2,1)}, bf16[2176,1,128]{2,0,1:T(8,128)(2,1)}, u32[]{:S(2)}, u32[]{:S(2)}) %collective-permute-start) | collective-permute-done | bytes 557088 | tf_op jit(solution)/shard_map/ppermute | solution.py:19
  40.8 5.6 %copy.62 = bf16[2176,1,128]{2,1,0:T(2,128)(2,1)S(1)} copy(bf16[2176,1,128]{2,0,1:T(8,128)(2,1)} %collective-permute-done) | data formatting | bytes 1114112 | tf_op jit(solution)/shard_map/ppermute | solution.py:19
  46.4 5.6 %copy.63 = bf16[2176,1,128]{2,1,0:T(2,128)(2,1)S(1)} copy(bf16[2176,1,128]{2,0,1:T(8,128)(2,1)} %collective-permute-done.1) | data formatting | bytes 1114112 | tf_op jit(solution)/shard_map/ppermute | solution.py:21
  52.0 3.5 %maximum_convert_fusion = f32[2176,4,128]{2,1,0:T(4,128)S(1)} fusion(bf16[2176,1,128]{2,1,0:T(2,128)(2,1)S(1)} %copy.63, bf16[2176,2,128]{2,1,0:T(2,128)(2,1)S(1)} %copy-done.2, bf16[2176,1,128]{2,1,0:T(2,128)(2,1)S(1)} %copy.62), kind=kLoop, calls=%fused_computation.14 | loop fusion | flops 6684672 | bytes 6684672 | tf_op jit(solution)/shard_map/convert_element_type | solution.py:100
  55.6 3.1 %fusion.89 = (f32[2,128]{1,0:T(2,128)S(1)}, f32[2176,2,128]{2,1,0:T(2,128)S(1)}) fusion(f32[2176,2,130]{2,1,0:T(2,128)S(1)} %maximum_convert_fusion.1, f32[2176,4,128]{2,1,0:T(4,128)S(1)} %maximum_convert_fusion), kind=kLoop, calls=%fused_computation.153 | loop fusion | flops 3342080 | bytes 11142144 | tf_op jit(solution)/shard_map/reduce_sum | solution.py:42
  58.9 6.5 %gather_fusion = f32[16,256,2,128]{3,2,1,0:T(2,128)} fusion(f32[2176,2,128]{2,1,0:T(2,128)S(1)} %bitcast.241, s32[16]{0:T(128)S(1)} %fusion.79), kind=kCustom, calls=%fused_computation.6 | custom fusion | bytes 8388800 | tf_op jit(solution)/shard_map/vmap()/gather | solution.py:43
  65.3 3.0 %convolution_bitcast_fusion = f32[16,256,2,128]{1,3,2,0:T(8,128)S(1)} fusion(f32[16,256,2,128]{3,2,1,0:T(2,128)} %gather_fusion, f32[256]{0:T(256)S(1)} %multiply_subtract_fusion, bf16[128,256]{1,0:T(8,128)(2,1)S(1)} %get-tuple-element.47, bf16[128,256]{1,0:T(8,128)(2,1)S(1)} %get-tuple-element.48), kind=kOutput, calls=%fused_computation.16 | convolution fusion | flops 539230208 | bytes 8520704 | tf_op jit(solution)/shard_map/ft,btxy->bfxy/dot_general | solution.py:45
  68.3 2.5 %fusion.91 = (f32[16,128,2,128]{1,3,2,0:T(8,128)}, f32[16,128,2,128]{1,3,2,0:T(8,128)}) fusion(f32[16,256,2,128]{1,3,2,0:T(8,128)S(1)} %convolution_bitcast_fusion), kind=kLoop, calls=%fused_computation.154 | loop fusion | bytes 8388608 | tf_op jit(solution)/shard_map/slice | solution.py:50
  70.9 2.4 %copy.70 = f32[16,128,2,128]{3,0,2,1:T(8,128)S(1)} copy(f32[16,128,2,128]{1,3,2,0:T(8,128)} %get-tuple-element.27) | data formatting | bytes 4194304 | tf_op jit(solution)/shard_map/slice | solution.py:50
  73.3 3.9 %copy.72 = f32[16,128,2,128]{3,0,2,1:T(8,128)} copy(f32[16,128,2,128]{1,3,2,0:T(8,128)} %get-tuple-element.28) | data formatting | bytes 4194304 | tf_op jit(solution)/shard_map/slice | solution.py:51
  77.8 3.2 %gather_fusion.4 = f32[64,16,2,128]{3,1,2,0:T(8,128)} fusion(f32[16,128,2,128]{3,0,2,1:T(8,128)} %copy.72, s32[1024]{0:T(1024)S(1)} %get-tuple-element.50), kind=kCustom, calls=%fused_computation.3.clone | custom fusion | bytes 2097408 | tf_op jit(solution)/shard_map/jit(_take)/gather | solution.py:56
  82.6 3.2 %gather_fusion.3 = f32[64,16,2,128]{3,1,2,0:T(8,128)} fusion(f32[16,128,2,128]{3,0,2,1:T(8,128)} %copy.72, s32[1024]{0:T(1024)S(1)} %pad_clamp_fusion.2), kind=kCustom, calls=%fused_computation.2.clone | custom fusion | bytes 2097408 | tf_op jit(solution)/shard_map/jit(_take)/gather | solution.py:54
  85.8 2.2 %gather_fusion.6 = f32[64,16,2,128]{3,1,2,0:T(8,128)S(1)} fusion(f32[16,128,2,128]{3,0,2,1:T(8,128)} %copy.72, s32[1024]{0:T(1024)S(1)} %get-tuple-element.49), kind=kCustom, calls=%fused_computation.5.clone | custom fusion | bytes 2097408 | tf_op jit(solution)/shard_map/jit(_take)/gather | solution.py:58
  88.0 2.2 %gather_fusion.5 = f32[64,16,2,128]{3,1,2,0:T(8,128)S(1)} fusion(f32[16,128,2,128]{3,0,2,1:T(8,128)} %copy-done, s32[1024]{0:T(1024)S(1)} %get-tuple-element.49), kind=kCustom, calls=%fused_computation.4.clone | custom fusion | bytes 2097408 | tf_op jit(solution)/shard_map/jit(_take)/gather | solution.py:57
  90.2 2.4 %fusion.23 = (f32[16,64,2,128]{3,0,2,1:T(8,128)S(1)}, f32[16,64,2,128]{3,0,2,1:T(8,128)S(1)}) fusion(f32[64,16,2,128]{3,1,2,0:T(8,128)} %gather_fusion.4, f32[64,16,2,128]{3,1,2,0:T(8,128)} %gather_fusion.3, f32[64,16,2,128]{3,1,2,0:T(8,128)S(1)} %gather_fusion.2, f32[64,16,2,128]{3,1,2,0:T(8,128)} %gather_fusion.1, f32[2,128]{1,0:T(2,128)S(1)} %copy-done.3, ...), kind=kLoop, calls=%fused_computation.43 | loop fusion | flops 3145728 | bytes 6292608 | tf_op jit(solution)/shard_map/mul | solution.py:59
  98.8 22.9 %reduce-scatter.4.cloned.1.call-done = f32[16,512]{1,0:T(8,128)} async-done(((f32[64,512]{1,0:T(8,128)}), f32[16,512]{1,0:T(8,128)}) %reduce-scatter.4.cloned.1.call-update) | async-done | bytes 32784
  122.7 45.4 %all-gather = f32[128,2,16,16]{3,2,0,1:T(8,128)} all-gather(f32[16,2,16,16]{3,2,0,1:T(8,128)S(1)} %copy.120), channel_id=2, replica_groups=mesh['space'=8,'freq'=4] {'space'}, dimensions={0}, use_global_device_ids=true | all-gather | bytes 294912 | tf_op jit(solution)/shard_map/all_gather | solution.py:109
  168.1 1.8 reduce_sum.83
  176.1 5.2 %all_gather.15 = f32[64,2,16]{2,0,1:T(8,128)S(1)} all-gather(f32[16,2,16]{2,0,1:T(8,128)S(1)} %pad_maximum_fusion.2), channel_id=1, replica_groups=mesh['space'=8,'freq'=4] {'freq'}, dimensions={0}, use_global_device_ids=true | all-gather | bytes 10240 | tf_op jit(solution)/shard_map/all_gather | solution.py:112
  186.0 5.1 %all-gather.1 = f32[4,16,2]{1,2,0:T(2,128)S(1)} all-gather(f32[1,16,2]{1,2,0:T(2,128)S(1)} %maximum_bitcast_fusion.2), channel_id=1, replica_groups=mesh['space'=8,'freq'=4] {'freq'}, dimensions={0}, use_global_device_ids=true | all-gather | bytes 640 | tf_op jit(solution)/shard_map/all_gather | solution.py:113
  (95 shorter events, 34.9 us)
Async XLA Ops:
  7.2 114.6 %reduce-scatter.4.cloned.1.call-start = ((), (), s32[]{:S(2)}) async-start(), calls=%async_computation.1 | async-start | bytes 163840
  10.9 8.7 %copy-start.1 = (bf16[2176,2,128]{2,1,0:T(2,128)(2,1)S(1)}, bf16[2176,2,128]{2,1,0:T(2,128)(2,1)}, u32[]{:S(2)}) copy-start(bf16[2176,2,128]{2,1,0:T(2,128)(2,1)} %param.7) | copy-start | bytes 3342340
  11.8 29.0 %collective-permute-start = (bf16[2176,1,128]{2,0,1:T(8,128)(2,1)}, bf16[2176,1,128]{2,0,1:T(8,128)(2,1)}, u32[]{:S(2)}, u32[]{:S(2)}) collective-permute-start(bf16[2176,1,128]{2,0,1:T(8,128)(2,1)} %copy.121), channel_id=1, source_target_pairs={{0,4},{4,8},{8,12},{12,16},{16,20},{20,24},{24,28},{1,5},{5,9},{9,... | collective-permute-start | bytes 1671176 | tf_op jit(solution)/shard_map/ppermute | solution.py:19
  18.4 28.0 %collective-permute-start.1 = (bf16[2176,1,128]{2,0,1:T(8,128)(2,1)}, bf16[2176,1,128]{2,0,1:T(8,128)(2,1)}, u32[]{:S(2)}, u32[]{:S(2)}) collective-permute-start(bf16[2176,1,128]{2,0,1:T(8,128)(2,1)} %copy.122), channel_id=1, source_target_pairs={{4,0},{8,4},{12,8},{16,12},{20,16},{24,20},{28,24},{5,1},{9,5},{13... | collective-permute-start | bytes 1671176 | tf_op jit(solution)/shard_map/ppermute | solution.py:21
  21.8 6.3 %copy-start.5 = (s32[16]{0:T(128)S(1)}, s32[16]{0:T(128)}, u32[]{:S(2)}) copy-start(s32[16]{0:T(128)} %param.10) | copy-start | bytes 196
  21.8 7.5 %copy-start.4 = (s32[64,2]{0,1:T(2,128)S(1)}, s32[64,2]{0,1:T(2,128)}, u32[]{:S(2)}) copy-start(s32[64,2]{0,1:T(2,128)} %param.11) | copy-start | bytes 1540
  23.1 6.3 %collective-permute-start.2 = (bf16[2176,2,1]{0,1,2:T(2,128)(2,1)S(1)}, bf16[2176,2,1]{0,1,2:T(2,128)(2,1)S(1)}, u32[]{:S(2)}, u32[]{:S(2)}) collective-permute-start(bf16[2176,2,1]{0,1,2:T(2,128)(2,1)S(1)} %copy.123), channel_id=1, source_target_pairs={{0,1},{1,2},{2,3},{4,5},{5,6},{6,7},{8,9},{9,10},{10,11},{12,13},{... | collective-permute-start | bytes 26120 | tf_op jit(solution)/shard_map/ppermute | solution.py:19
  25.9 5.1 %collective-permute-start.3 = (bf16[2176,2,1]{0,1,2:T(2,128)(2,1)S(1)}, bf16[2176,2,1]{0,1,2:T(2,128)(2,1)S(1)}, u32[]{:S(2)}, u32[]{:S(2)}) collective-permute-start(bf16[2176,2,1]{0,1,2:T(2,128)(2,1)S(1)} %copy.124), channel_id=1, source_target_pairs={{1,0},{2,1},{3,2},{5,4},{6,5},{7,6},{9,8},{10,9},{11,10},{13,12},{... | collective-permute-start | bytes 26120 | tf_op jit(solution)/shard_map/ppermute | solution.py:21
  38.7 13.4 %copy-start.2 = (bf16[2176,2,128]{2,1,0:T(2,128)(2,1)S(1)}, bf16[2176,2,128]{2,1,0:T(2,128)(2,1)}, u32[]{:S(2)}) copy-start(bf16[2176,2,128]{2,1,0:T(2,128)(2,1)} %param.8) | copy-start | bytes 3342340
  73.3 7.7 %copy-start = (f32[16,128,2,128]{3,0,2,1:T(8,128)}, f32[16,128,2,128]{3,0,2,1:T(8,128)S(1)}, u32[]{:S(2)}) copy-start(f32[16,128,2,128]{3,0,2,1:T(8,128)S(1)} %copy.70) | copy-start | bytes 6291460
  85.8 4.4 %copy-start.3 = (f32[2,128]{1,0:T(2,128)S(1)}, f32[2,128]{1,0:T(2,128)}, u32[]{:S(2)}) copy-start(f32[2,128]{1,0:T(2,128)} %param.9) | copy-start | bytes 3076
Sparse Core Ops, SparseCore 0:
  99.0 22.7 reduce-scatter.3
